TPU v7x, 32 devices: a whole 2x2x4 slice. The times are simulated.
32 devices in a mesh: ka: 4 (over y, x), rp: 8 (over z, core).
Axes of the slice: x: 2, y: 2, z: 4, core: 2. Of those that a mesh axis runs over, the one named last changes fastest.
Arguments:
- coupling_table: bfloat16 [512, 256, 1024], P('ka', 'rp'), may hold values from -0.016479492 to 0.016479492
- k_points: int32 [3, 2048], P(None, 'ka'), may hold values from 0 to 15
- re_vectors: int32 [3, 512], replicated, may hold values from -6 to 6
- rp_vectors: int32 [3, 256], P(None, 'rp'), may hold values from -6 to 6
- q_points: int32 [3, 2], replicated, may hold values from 0 to 15
Outputs:
- bloch_coupling: float32 [2048, 2048], P(('ka', 'rp'))
All inputs are finite; a program needn't handle non-finite values.
Results may differ from a plain program's by a relative error of at most 0.0022.
Values may be sent and summed in bfloat16 or wider, within the bound.
A program may use at most 64 MiB of HBM per device.

v0:
```python
import math
import jax
import jax.numpy as jnp
from jax import lax
from jax.sharding import PartitionSpec as P

NKG = 16


def phases(left, right):
    nested = (
        left[0][:, None] * right[0][None, :]
        + left[1][:, None] * right[1][None, :]
        + left[2][:, None] * right[2][None, :]
    )
    wrapped = jnp.mod(nested, NKG)
    angles = wrapped.astype(jnp.float32) * (2.0 * math.pi / NKG)
    return (jnp.cos(angles), jnp.sin(angles))


def per_device(coupling_table, k_points, re_vectors, rp_vectors, q_points):
    high = lax.Precision.HIGHEST
    local_rp = coupling_table.shape[1]
    entries = coupling_table.shape[2] // 2
    waves = q_points.shape[1]
    q_cos, q_sin = phases(q_points, rp_vectors)
    k_cos, k_sin = phases(k_points, re_vectors)
    k_cos = k_cos.astype(jnp.bfloat16)
    k_sin = k_sin.astype(jnp.bfloat16)
    local_re = coupling_table.shape[0]
    values = coupling_table.astype(jnp.float32).reshape(local_re, local_rp, 2, entries)
    real_in = values[:, :, 0, :]
    imag_in = values[:, :, 1, :]
    real_mid = jnp.einsum("qr,erm->eqm", q_cos, real_in, precision=high) - jnp.einsum(
        "qr,erm->eqm", q_sin, imag_in, precision=high
    )
    imag_mid = jnp.einsum("qr,erm->eqm", q_sin, real_in, precision=high) + jnp.einsum(
        "qr,erm->eqm", q_cos, imag_in, precision=high
    )
    stacked = jnp.stack(
        [real_mid.reshape(local_re, waves * entries), imag_mid.reshape(local_re, waves * entries)],
        axis=0,
    )
    reduced = lax.psum_scatter(stacked, "rp", scatter_dimension=2, tiled=True)
    fragment = lax.all_gather(reduced, "ka", axis=1, tiled=True)
    cos_part = k_cos.astype(jnp.float32)
    sin_part = k_sin.astype(jnp.float32)
    real_add = jnp.dot(
        cos_part, fragment[0], precision=high, preferred_element_type=jnp.float32
    ) - jnp.dot(sin_part, fragment[1], precision=high, preferred_element_type=jnp.float32)
    imag_add = jnp.dot(
        sin_part, fragment[0], precision=high, preferred_element_type=jnp.float32
    ) + jnp.dot(cos_part, fragment[1], precision=high, preferred_element_type=jnp.float32)
    combined = jnp.stack([real_add, imag_add], axis=1)
    moved = lax.all_to_all(combined, "rp", split_axis=0, concat_axis=2, tiled=True)
    return moved.reshape(moved.shape[0], 2 * waves * entries)


def solution(mesh):
    placed = (P("ka", "rp", None), P(None, "ka"), P(), P(None, "rp"), P())
    return jax.shard_map(
        per_device, mesh=mesh, in_specs=placed, out_specs=P(("ka", "rp"), None), check_vma=False
    )
```

profile of v0, /device:TPU:0, one launch (start us, length us, event | category | flops | bytes accessed | tf_op | source)
XLA Modules:
  0.0 146.7 jit_solution(4808768817966968522)
XLA Ops:
  6.5 0.0 reduce-scatter.2.cloned.1.call-start
  6.5 0.8 slice_bitcast_fusion.8
  7.3 1.0 slice_reduce_fusion.2
  8.3 12.1 %copy.11 = bf16[128,32,1024]{0,2,1:T(8,128)(2,1)} copy(bf16[128,32,1024]{2,1,0:T(8,128)(2,1)} %param.5) | data formatting | bytes 16777216 | tf_op args[0]
  20.4 5.9 %fusion.52 = (bf16[128,32,1,512]{0,3,2,1:T(8,128)(2,1)}, bf16[128,32,1,512]{0,3,2,1:T(8,128)(2,1)}) fusion(bf16[128,32,2,512]{0,3,2,1:T(8,128)(2,1)} %bitcast.65), kind=kLoop, calls=%fused_computation.64 | loop fusion | bytes 16777216 | tf_op jit(solution)/shard_map/slice | solution.py:32
  26.3 8.0 %copy.17 = bf16[128,32,1,512]{3,1,0,2:T(8,128)(2,1)} copy(bf16[128,32,1,512]{0,3,2,1:T(8,128)(2,1)} %get-tuple-element.11) | data formatting | bytes 8388608
  34.3 0.1 fusion.50
  34.4 8.0 %copy.16 = bf16[128,32,1,512]{3,1,0,2:T(8,128)(2,1)} copy(bf16[128,32,1,512]{0,3,2,1:T(8,128)(2,1)} %get-tuple-element.10) | data formatting | bytes 8388608
  42.4 4.1 %fusion.2 = f32[2,128,512]{2,0,1:T(2,128)S(1)} fusion(bf16[128,32,1,512]{3,1,0,2:T(8,128)(2,1)} %copy.17, f32[2,32]{1,0:T(2,128)S(1)} %get-tuple-element.8), kind=kOutput, calls=%fused_computation.2 | convolution fusion | flops 50331648 | bytes 4718848 | tf_op jit(solution)/shard_map/qr,erm->eqm/dot_general | solution.py:34
  46.5 0.0 copy-done
  46.5 1.8 %fusion = f32[2,128,512]{2,0,1:T(2,128)S(1)} fusion(bf16[128,32,1,512]{3,1,0,2:T(8,128)(2,1)S(1)} %copy-done, f32[2,32]{1,0:T(2,128)S(1)} %cos.7), kind=kOutput, calls=%fused_computation | convolution fusion | flops 50331648 | bytes 4718848 | tf_op jit(solution)/shard_map/qr,erm->eqm/dot_general | solution.py:37
  48.3 0.0 copy-done.1
  48.3 1.8 %fusion.11 = f32[128,2,512]{2,1,0:T(2,128)S(1)} fusion(f32[2,128,512]{2,0,1:T(2,128)S(1)} %fusion.2, bf16[128,32,1,512]{3,1,0,2:T(8,128)(2,1)S(1)} %copy-done.1, f32[2,32]{1,0:T(2,128)S(1)} %cos.7), kind=kOutput, calls=%fused_computation.12 | convolution fusion | flops 50462720 | bytes 5243136 | tf_op jit(solution)/shard_map/qr,erm->eqm/dot_general | solution.py:34
  50.1 0.5 stack_reshape.6
  50.6 0.0 copy-start.2
  50.6 0.0 copy-start.3
  50.6 3.9 %fusion.17 = f32[128,2,512]{2,1,0:T(2,128)S(1)} fusion(f32[2,128,512]{2,0,1:T(2,128)S(1)} %fusion, bf16[128,32,1,512]{3,1,0,2:T(8,128)(2,1)} %copy.16, f32[2,32]{1,0:T(2,128)S(1)} %get-tuple-element.8), kind=kOutput, calls=%fused_computation.14 | convolution fusion | flops 50462720 | bytes 5243136 | tf_op jit(solution)/shard_map/qr,erm->eqm/dot_general | solution.py:37
  54.5 0.5 stack_reshape.7
  55.0 1.0 pad_maximum_fusion
  56.0 0.0 reduce-scatter.2.cloned.1.call-update
  56.1 0.0 copy-done.2
  56.1 0.0 copy-done.3
  56.1 35.4 %reduce-scatter.2.cloned.1.call-done = f32[2,128,128]{2,1,0:T(8,128)} async-done(((f32[2,128,1024]{2,1,0:T(8,128)}), f32[2,128,128]{2,1,0:T(8,128)}) %reduce-scatter.2.cloned.1.call-update) | async-done | bytes 131088 | tf_op jit(solution)/shard_map/reduce_scatter | solution.py:44
  91.5 10.5 %all_gather.3 = f32[2,512,128]{2,1,0:T(8,128)S(1)} all-gather(f32[2,128,128]{2,1,0:T(8,128)} %reduce-scatter.2.cloned.1.call-done), channel_id=1, replica_groups=mesh['ka'=4,'rp'=8] {'ka'}, dimensions={1}, use_global_device_ids=true | all-gather | bytes 655360 | tf_op jit(solution)/shard_map/all_gather | solution.py:45
  102.0 4.5 %fusion.25 = f32[512,128]{1,0:T(8,128)S(1)} fusion(s32[512]{0:T(512)S(1)} %bitcast.84, s32[512]{0:T(512)S(1)} %bitcast.72, s32[512]{0:T(512)S(1)} %bitcast.88, s32[512]{0:T(512)S(1)} %bitcast.76, s32[512]{0:T(512)S(1)} %bitcast.80, s32[512]{0:T(512)S(1)} %bitcast.68, f32[2,512,128]{2,1,0:T(8,128)S(1)} %all_gather.3), kind=kOutput, calls=%fused_computation.27 | convolution fusion | flops 407633920 | bytes 536576 | tf_op jit(solution)/shard_map/dot_general | solution.py:48
  106.5 4.6 %fusion.26 = f32[512,128]{1,0:T(8,128)S(1)} fusion(s32[512]{0:T(512)S(1)} %bitcast.85, s32[512]{0:T(512)S(1)} %bitcast.73, s32[512]{0:T(512)S(1)} %bitcast.89, s32[512]{0:T(512)S(1)} %bitcast.77, s32[512]{0:T(512)S(1)} %bitcast.81, s32[512]{0:T(512)S(1)} %bitcast.69, f32[2,512,128]{2,1,0:T(8,128)S(1)} %all_gather.3), kind=kOutput, calls=%fused_computation.28 | convolution fusion | flops 407633920 | bytes 536576 | tf_op jit(solution)/shard_map/dot_general | solution.py:51
  111.1 4.8 %fusion.21 = f32[512,1,128]{2,0,1:T(8,128)S(1)} fusion(f32[512,128]{1,0:T(8,128)S(1)} %fusion.25, s32[512]{0:T(512)S(1)} %bitcast.86, s32[512]{0:T(512)S(1)} %bitcast.74, s32[512]{0:T(512)S(1)} %bitcast.90, s32[512]{0:T(512)S(1)} %bitcast.78, s32[512]{0:T(512)S(1)} %bitcast.82, s32[512]{0:T(512)S(1)} %bitcast.70, f32[2,512,128]{2,1,0:T(8,128)S(1)} %all_gather.3), kind=kOutput, calls=%fused_computation.18 | convolution fusion | flops 407699456 | bytes 798720 | tf_op jit(solution)/shard_map/dot_general | solution.py:50
  115.9 4.5 %fusion.20 = f32[512,1,128]{2,0,1:T(8,128)S(1)} fusion(f32[512,128]{1,0:T(8,128)S(1)} %fusion.26, s32[512]{0:T(512)S(1)} %bitcast.87, s32[512]{0:T(512)S(1)} %bitcast.75, s32[512]{0:T(512)S(1)} %bitcast.91, s32[512]{0:T(512)S(1)} %bitcast.79, s32[512]{0:T(512)S(1)} %bitcast.83, s32[512]{0:T(512)S(1)} %bitcast.71, f32[2,512,128]{2,1,0:T(8,128)S(1)} %all_gather.3), kind=kOutput, calls=%fused_computation.16 | convolution fusion | flops 407699456 | bytes 798720 | tf_op jit(solution)/shard_map/dot_general | solution.py:53
  120.4 0.4 copy.14
  120.8 17.7 %all_to_all.15 = f32[512,2,128]{2,1,0:T(2,128)S(1)} all-to-all(f32[512,2,128]{2,1,0:T(2,128)S(1)} %copy.14), channel_id=1, replica_groups=mesh['ka'=4,'rp'=8] {'rp'}, dimensions={0} | all-to-all | bytes 1048576 | tf_op jit(solution)/shard_map/all_to_all | solution.py:55
  138.6 0.3 copy.15
  138.9 1.0 copy.20
  (6 shorter events, 0.1 us)
Async XLA Ops:
  6.5 85.0 %reduce-scatter.2.cloned.1.call-start = ((), (), s32[]{:S(2)}) async-start(), calls=%async_computation.2 | async-start | bytes 1179648 | tf_op jit(solution)/shard_map/reduce_scatter | solution.py:44
  42.4 4.1 %copy-start = (bf16[128,32,1,512]{3,1,0,2:T(8,128)(2,1)S(1)}, bf16[128,32,1,512]{3,1,0,2:T(8,128)(2,1)}, u32[]{:S(2)}) copy-start(bf16[128,32,1,512]{3,1,0,2:T(8,128)(2,1)} %copy.17) | copy-start | bytes 12582916
  42.4 5.9 %copy-start.1 = (bf16[128,32,1,512]{3,1,0,2:T(8,128)(2,1)S(1)}, bf16[128,32,1,512]{3,1,0,2:T(8,128)(2,1)}, u32[]{:S(2)}) copy-start(bf16[128,32,1,512]{3,1,0,2:T(8,128)(2,1)} %copy.16) | copy-start | bytes 12582916
  50.6 5.5 %copy-start.2 = (s32[3,512]{1,0:T(4,128)S(1)}, s32[3,512]{1,0:T(4,128)}, u32[]{:S(2)}) copy-start(s32[3,512]{1,0:T(4,128)} %param.6) | copy-start | bytes 18436
  50.6 5.5 %copy-start.3 = (s32[3,512]{1,0:T(4,128)S(1)}, s32[3,512]{1,0:T(4,128)}, u32[]{:S(2)}) copy-start(s32[3,512]{1,0:T(4,128)} %param.7) | copy-start | bytes 18436
Sparse Core Ops, SparseCore 0:
  56.2 35.2 reduce-scatter.1
where the time goes:
time: 148 us; the launch traced here: 147 us
  local copies, waits for them, and re-layouts  38.3 us (26%)
  waiting for transfers between devices  35.4 us (24%)
  matrix products  30 us (20%)
  blocking collectives  28.2 us (19%)
  between operations  13.5 us (9%)
    reduce_scatter x1, waiting for transfers between devices, per_device(): reduced = lax.psum_scatter(stacked, 'rp', scatter_dimension=2, tiled=True)  35.4 us
    unnamed x12, local copies, waits for them, and re-layouts  29 us
    all_to_all x1, blocking collectives, per_device(): lax.all_to_all(combined, 'rp', split_axis=0, concat_axis=2, tiled=True)  17.7 us
    all_gather x1, blocking collectives, per_device(): fragment = lax.all_gather(reduced, 'ka', axis=1, tiled=True)  10.5 us
    slice x1, local copies, waits for them, and re-layouts, per_device(): real_in = values[:, :, 0, :]  5.88 us
    dot_general x1, matrix products, per_device(): jnp.dot(sin_part, fragment[1], precision=high, preferred_element_type=jnp...  4.77 us
    dot_general x1, matrix products, per_device(): jnp.dot(sin_part, fragment[0], precision=high, preferred_element_type=jnp...  4.55 us
    dot_general x1, matrix products, per_device(): jnp.dot(cos_part, fragment[0], precision=high, preferred_element_type=jnp...  4.52 us
  transfers between devices with their start and end apart: 1, of which 1 were waited for; matrix products, arithmetic and copies ran while one was open for 0% of the time, Pallas kernels for 0%

commit v1 on v0

--- a/solution.py
+++ b/solution.py
@@ -5,6 +5,18 @@
 from jax.sharding import PartitionSpec as P
 
 NKG = 16
+
+
+def split_up(array, dim, size):
+    shape = array.shape
+    blocks = array.reshape(*shape[:dim], size, shape[dim] // size, *shape[dim + 1 :])
+    return jnp.moveaxis(blocks, dim, 0)
+
+
+def joined_along(blocks, dim):
+    shape = list(blocks.shape[1:])
+    shape[dim] *= blocks.shape[0]
+    return jnp.moveaxis(blocks, 0, dim).reshape(shape)
 
 
 def phases(left, right):
@@ -52,7 +64,14 @@
         sin_part, fragment[0], precision=high, preferred_element_type=jnp.float32
     ) + jnp.dot(cos_part, fragment[1], precision=high, preferred_element_type=jnp.float32)
     combined = jnp.stack([real_add, imag_add], axis=1)
-    moved = lax.all_to_all(combined, "rp", split_axis=0, concat_axis=2, tiled=True)
+    peers, here = (lax.axis_size("rp"), lax.axis_index("rp"))
+    parts = split_up(combined, 0, peers)
+    outs = [parts[here]]
+    for step in range(1, peers):
+        sent = parts[here ^ step]
+        outs.append(lax.ppermute(sent, "rp", [(i, i ^ step) for i in range(peers)]))
+    parts = jnp.stack(outs)[here ^ jnp.arange(peers)]
+    moved = joined_along(parts, 2)
     return moved.reshape(moved.shape[0], 2 * waves * entries)
 
 

time: 148 us -> 143 us (0.966)
  blocking collectives: 28.2 us -> 10.2 us
  waiting for transfers between devices: 35.4 us -> 43 us
  starting transfers between devices: 0.01 us -> 5.92 us
    all_to_all x1 -> x0, blocking collectives: 17.7 us -> none  [per_device(): lax.all_to_all(combined, 'rp', split_axis=0, concat_axis=2, tiled=True)]
    ppermute x0 -> x7, waiting for transfers between devices: none -> 7.34 us  [per_device(): outs.append(lax.ppermute(sent, 'rp', [(i, i ^ step) for i in range(peers)]))]
    ppermute x0 -> x7, starting transfers between devices: none -> 5.92 us  [per_device(): outs.append(lax.ppermute(sent, 'rp', [(i, i ^ step) for i in range(peers)]))]
    unnamed x12 -> x18, local copies, waits for them, and re-layouts: 29 us -> 29 us
  transfers between devices with their start and end apart: 1 -> 8, of which waited for: 1 -> 6; matrix products, arithmetic and copies ran while one was open for 0% -> 0% of each run, Pallas kernels for 0% -> 0%
where the time goes in v1:
time: 143 us; the launch traced here: 142 us
  waiting for transfers between devices  43 us (30%)
  local copies, waits for them, and re-layouts  38.5 us (27%)
  matrix products  30 us (21%)
  between operations  13.6 us (10%)
  blocking collectives  10.2 us (7%)
  starting transfers between devices  5.92 us (4%)
    reduce_scatter x1, waiting for transfers between devices, per_device(): reduced = lax.psum_scatter(stacked, 'rp', scatter_dimension=2, tiled=True)  35.7 us
    unnamed x18, local copies, waits for them, and re-layouts  29 us
    all_gather x1, blocking collectives, per_device(): fragment = lax.all_gather(reduced, 'ka', axis=1, tiled=True)  10.2 us
    ppermute x7, waiting for transfers between devices, per_device(): outs.append(lax.ppermute(sent, 'rp', [(i, i ^ step) for i in range(peers)]))  7.34 us
    ppermute x7, starting transfers between devices, per_device(): outs.append(lax.ppermute(sent, 'rp', [(i, i ^ step) for i in range(peers)]))  5.92 us
    slice x1, local copies, waits for them, and re-layouts, per_device(): real_in = values[:, :, 0, :]  5.88 us
    dot_general x1, matrix products, per_device(): jnp.dot(cos_part, fragment[1], precision=high, preferred_element_type=jnp...  4.74 us
    dot_general x1, matrix products, per_device(): jnp.dot(sin_part, fragment[1], precision=high, preferred_element_type=jnp...  4.56 us
  transfers between devices with their start and end apart: 8, of which 6 were waited for; matrix products, arithmetic and copies ran while one was open for 0% of the time, Pallas kernels for 0%

profile of v1, /device:TPU:0, one launch (start us, length us, event | category | flops | bytes accessed | tf_op | source)
XLA Modules:
  0.0 142.5 jit_solution(16367512560348488426)
XLA Ops:
  6.5 0.8 slice_bitcast_fusion.8
  7.3 1.0 slice_reduce_fusion.2
  8.3 12.1 %copy.7 = bf16[128,32,1024]{0,2,1:T(8,128)(2,1)} copy(bf16[128,32,1024]{2,1,0:T(8,128)(2,1)} %param.5) | data formatting | bytes 16777216 | tf_op args[0]
  20.4 5.9 %fusion.67 = (bf16[128,32,1,512]{0,3,2,1:T(8,128)(2,1)}, bf16[128,32,1,512]{0,3,2,1:T(8,128)(2,1)}) fusion(bf16[128,32,2,512]{0,3,2,1:T(8,128)(2,1)} %bitcast.91), kind=kLoop, calls=%fused_computation.104 | loop fusion | bytes 16777216 | tf_op jit(solution)/shard_map/slice | solution.py:44
  26.3 7.9 %copy.12 = bf16[128,32,1,512]{3,1,0,2:T(8,128)(2,1)} copy(bf16[128,32,1,512]{0,3,2,1:T(8,128)(2,1)} %get-tuple-element.11) | data formatting | bytes 8388608
  34.2 0.1 fusion.65
  34.4 8.0 %copy.11 = bf16[128,32,1,512]{3,1,0,2:T(8,128)(2,1)} copy(bf16[128,32,1,512]{0,3,2,1:T(8,128)(2,1)} %get-tuple-element.10) | data formatting | bytes 8388608
  42.4 4.1 %fusion.2 = f32[2,128,512]{2,0,1:T(2,128)S(1)} fusion(bf16[128,32,1,512]{3,1,0,2:T(8,128)(2,1)} %copy.12, f32[2,32]{1,0:T(2,128)S(1)} %get-tuple-element.8), kind=kOutput, calls=%fused_computation.3 | convolution fusion | flops 50331648 | bytes 4718848 | tf_op jit(solution)/shard_map/qr,erm->eqm/dot_general | solution.py:46
  46.5 1.8 %fusion = f32[2,128,512]{2,0,1:T(2,128)S(1)} fusion(bf16[128,32,1,512]{3,1,0,2:T(8,128)(2,1)S(1)} %copy-done, f32[2,32]{1,0:T(2,128)S(1)} %cos.7), kind=kOutput, calls=%fused_computation.1 | convolution fusion | flops 50331648 | bytes 4718848 | tf_op jit(solution)/shard_map/qr,erm->eqm/dot_general | solution.py:49
  48.3 1.8 %fusion.11 = f32[128,2,512]{2,1,0:T(2,128)S(1)} fusion(f32[2,128,512]{2,0,1:T(2,128)S(1)} %fusion.2, bf16[128,32,1,512]{3,1,0,2:T(8,128)(2,1)S(1)} %copy-done.1, f32[2,32]{1,0:T(2,128)S(1)} %cos.7), kind=kOutput, calls=%fused_computation.13 | convolution fusion | flops 50462720 | bytes 5243136 | tf_op jit(solution)/shard_map/qr,erm->eqm/dot_general | solution.py:46
  50.1 0.5 stack_reshape.6
  50.5 3.9 %fusion.17 = f32[128,2,512]{2,1,0:T(2,128)S(1)} fusion(f32[2,128,512]{2,0,1:T(2,128)S(1)} %fusion, bf16[128,32,1,512]{3,1,0,2:T(8,128)(2,1)} %copy.11, f32[2,32]{1,0:T(2,128)S(1)} %get-tuple-element.8), kind=kOutput, calls=%fused_computation.15 | convolution fusion | flops 50462720 | bytes 5243136 | tf_op jit(solution)/shard_map/qr,erm->eqm/dot_general | solution.py:49
  54.5 0.5 stack_reshape.7
  54.9 1.0 pad_maximum_fusion
  56.1 35.7 %reduce-scatter.2.cloned.1.call-done = f32[2,128,128]{2,1,0:T(8,128)} async-done(((f32[2,128,1024]{2,1,0:T(8,128)}), f32[2,128,128]{2,1,0:T(8,128)}) %reduce-scatter.2.cloned.1.call-update) | async-done | bytes 131088 | tf_op jit(solution)/shard_map/reduce_scatter | solution.py:56
  91.8 10.2 %all_gather.3 = f32[2,512,128]{2,1,0:T(8,128)S(1)} all-gather(f32[2,128,128]{2,1,0:T(8,128)} %reduce-scatter.2.cloned.1.call-done), channel_id=1, replica_groups=mesh['ka'=4,'rp'=8] {'ka'}, dimensions={1}, use_global_device_ids=true | all-gather | bytes 655360 | tf_op jit(solution)/shard_map/all_gather | solution.py:57
  102.0 4.6 %fusion.24 = f32[512,128]{1,0:T(8,128)S(1)} fusion(s32[512]{0:T(512)S(1)} %bitcast.114, s32[512]{0:T(512)S(1)} %bitcast.102, s32[512]{0:T(512)S(1)} %bitcast.118, s32[512]{0:T(512)S(1)} %bitcast.106, s32[512]{0:T(512)S(1)} %bitcast.110, s32[512]{0:T(512)S(1)} %bitcast.98, f32[2,512,128]{2,1,0:T(8,128)S(1)} %all_gather.3), kind=kOutput, calls=%fused_computation.42 | convolution fusion | flops 407633920 | bytes 536576 | tf_op jit(solution)/shard_map/dot_general | solution.py:63
  106.5 4.5 %fusion.23 = f32[512,128]{1,0:T(8,128)S(1)} fusion(s32[512]{0:T(512)S(1)} %bitcast.115, s32[512]{0:T(512)S(1)} %bitcast.103, s32[512]{0:T(512)S(1)} %bitcast.119, s32[512]{0:T(512)S(1)} %bitcast.107, s32[512]{0:T(512)S(1)} %bitcast.111, s32[512]{0:T(512)S(1)} %bitcast.99, f32[2,512,128]{2,1,0:T(8,128)S(1)} %all_gather.3), kind=kOutput, calls=%fused_computation.41 | convolution fusion | flops 407633920 | bytes 536576 | tf_op jit(solution)/shard_map/dot_general | solution.py:60
  111.0 4.7 %convolution_add_fusion = f32[512,128]{1,0:T(8,128)S(1)} fusion(f32[512,128]{1,0:T(8,128)S(1)} %fusion.24, s32[512]{0:T(512)S(1)} %bitcast.116, s32[512]{0:T(512)S(1)} %bitcast.104, s32[512]{0:T(512)S(1)} %bitcast.120, s32[512]{0:T(512)S(1)} %bitcast.108, s32[512]{0:T(512)S(1)} %bitcast.112, s32[512]{0:T(512)S(1)} %bitcast.100, ...), kind=kOutput, calls=%fused_computation.32 | convolution fusion | flops 407699456 | bytes 798720 | tf_op jit(solution)/shard_map/dot_general | solution.py:65
  115.8 4.6 %convolution_subtract_fusion = f32[512,128]{1,0:T(8,128)S(1)} fusion(f32[512,128]{1,0:T(8,128)S(1)} %fusion.23, s32[512]{0:T(512)S(1)} %bitcast.117, s32[512]{0:T(512)S(1)} %bitcast.105, s32[512]{0:T(512)S(1)} %bitcast.121, s32[512]{0:T(512)S(1)} %bitcast.109, s32[512]{0:T(512)S(1)} %bitcast.113, s32[512]{0:T(512)S(1)} %bitcast.101, ...), kind=kOutput, calls=%fused_computation.33 | convolution fusion | flops 407699456 | bytes 798720 | tf_op jit(solution)/shard_map/dot_general | solution.py:62
  120.6 1.5 %collective-permute-start.1 = (f32[64,2,128]{2,0,1:T(8,128)S(1)}, f32[64,2,128]{2,0,1:T(8,128)S(1)}, u32[]{:S(2)}, u32[]{:S(2)}) collective-permute-start(f32[64,2,128]{2,0,1:T(8,128)S(1)} %get-tuple-element.15), channel_id=1, source_target_pairs={{0,2},{1,3},{2,0},{3,1},{4,6},{5,7},{6,4},{7,5},{8,10},{9,11},{10,... | collective-permute-start | bytes 196616 | tf_op jit(solution)/shard_map/ppermute | solution.py:72
  122.1 0.4 collective-permute-start.2
  122.5 2.5 %collective-permute-start.3 = (f32[64,2,128]{2,0,1:T(8,128)S(1)}, f32[64,2,128]{2,0,1:T(8,128)S(1)}, u32[]{:S(2)}, u32[]{:S(2)}) collective-permute-start(f32[64,2,128]{2,0,1:T(8,128)S(1)} %get-tuple-element.17), channel_id=1, source_target_pairs={{0,4},{1,5},{2,6},{3,7},{4,0},{5,1},{6,2},{7,3},{8,12},{9,13},{10,... | collective-permute-start | bytes 196616 | tf_op jit(solution)/shard_map/ppermute | solution.py:72
  125.0 0.9 collective-permute-start.5
  125.8 2.3 %collective-permute-done.1 = f32[64,2,128]{2,0,1:T(8,128)S(1)} collective-permute-done((f32[64,2,128]{2,0,1:T(8,128)S(1)}, f32[64,2,128]{2,0,1:T(8,128)S(1)}, u32[]{:S(2)}, u32[]{:S(2)}) %collective-permute-start.1) | collective-permute-done | bytes 65568 | tf_op jit(solution)/shard_map/ppermute | solution.py:72
  128.2 0.5 collective-permute-start.6
  128.7 0.3 collective-permute-done.3
  129.1 2.2 %collective-permute-done.5 = f32[64,2,128]{2,0,1:T(8,128)S(1)} collective-permute-done((f32[64,2,128]{2,0,1:T(8,128)S(1)}, f32[64,2,128]{2,0,1:T(8,128)S(1)}, u32[]{:S(2)}, u32[]{:S(2)}) %collective-permute-start.5) | collective-permute-done | bytes 65568 | tf_op jit(solution)/shard_map/ppermute | solution.py:72
  131.3 2.5 %collective-permute-done.6 = f32[64,2,128]{2,0,1:T(8,128)S(1)} collective-permute-done((f32[64,2,128]{2,0,1:T(8,128)S(1)}, f32[64,2,128]{2,0,1:T(8,128)S(1)}, u32[]{:S(2)}, u32[]{:S(2)}) %collective-permute-start.6) | collective-permute-done | bytes 65568 | tf_op jit(solution)/shard_map/ppermute | solution.py:72
  133.8 0.6 gather_fusion
  134.3 0.3 copy.10
  134.7 1.0 copy.15
  (29 shorter events, 0.4 us)
Async XLA Ops:
  6.5 85.3 %reduce-scatter.2.cloned.1.call-start = ((), (), s32[]{:S(2)}) async-start(), calls=%async_computation.1 | async-start | bytes 1179648 | tf_op jit(solution)/shard_map/reduce_scatter | solution.py:56
  42.4 4.1 %copy-start = (bf16[128,32,1,512]{3,1,0,2:T(8,128)(2,1)S(1)}, bf16[128,32,1,512]{3,1,0,2:T(8,128)(2,1)}, u32[]{:S(2)}) copy-start(bf16[128,32,1,512]{3,1,0,2:T(8,128)(2,1)} %copy.12) | copy-start | bytes 12582916
  42.4 5.9 %copy-start.1 = (bf16[128,32,1,512]{3,1,0,2:T(8,128)(2,1)S(1)}, bf16[128,32,1,512]{3,1,0,2:T(8,128)(2,1)}, u32[]{:S(2)}) copy-start(bf16[128,32,1,512]{3,1,0,2:T(8,128)(2,1)} %copy.11) | copy-start | bytes 12582916
  50.5 5.6 %copy-start.2 = (s32[3,512]{1,0:T(4,128)S(1)}, s32[3,512]{1,0:T(4,128)}, u32[]{:S(2)}) copy-start(s32[3,512]{1,0:T(4,128)} %param.6) | copy-start | bytes 18436
  50.5 5.6 %copy-start.3 = (s32[3,512]{1,0:T(4,128)S(1)}, s32[3,512]{1,0:T(4,128)}, u32[]{:S(2)}) copy-start(s32[3,512]{1,0:T(4,128)} %param.7) | copy-start | bytes 18436
  120.4 4.6 %collective-permute-start = (f32[64,2,128]{2,0,1:T(8,128)S(1)}, f32[64,2,128]{2,0,1:T(8,128)S(1)}, u32[]{:S(2)}, u32[]{:S(2)}) collective-permute-start(f32[64,2,128]{2,0,1:T(8,128)S(1)} %get-tuple-element.14), channel_id=1, source_target_pairs={{0,1},{1,0},{2,3},{3,2},{4,5},{5,4},{6,7},{7,6},{8,9},{9,8},{10,11... | collective-permute-start | bytes 196616 | tf_op jit(solution)/shard_map/ppermute | solution.py:72
  120.5 8.6 %collective-permute-start.4 = (f32[64,2,128]{2,0,1:T(8,128)S(1)}, f32[64,2,128]{2,0,1:T(8,128)S(1)}, u32[]{:S(2)}, u32[]{:S(2)}) collective-permute-start(f32[64,2,128]{2,0,1:T(8,128)S(1)} %get-tuple-element.19), channel_id=1, source_target_pairs={{0,5},{1,4},{2,7},{3,6},{4,1},{5,0},{6,3},{7,2},{8,13},{9,12},{10,... | collective-permute-start | bytes 196616 | tf_op jit(solution)/shard_map/ppermute | solution.py:72
  120.6 7.6 %collective-permute-start.1 = (f32[64,2,128]{2,0,1:T(8,128)S(1)}, f32[64,2,128]{2,0,1:T(8,128)S(1)}, u32[]{:S(2)}, u32[]{:S(2)}) collective-permute-start(f32[64,2,128]{2,0,1:T(8,128)S(1)} %get-tuple-element.15), channel_id=1, source_target_pairs={{0,2},{1,3},{2,0},{3,1},{4,6},{5,7},{6,4},{7,5},{8,10},{9,11},{10,... | collective-permute-start | bytes 196616 | tf_op jit(solution)/shard_map/ppermute | solution.py:72
  122.1 6.6 %collective-permute-start.2 = (f32[64,2,128]{2,0,1:T(8,128)S(1)}, f32[64,2,128]{2,0,1:T(8,128)S(1)}, u32[]{:S(2)}, u32[]{:S(2)}) collective-permute-start(f32[64,2,128]{2,0,1:T(8,128)S(1)} %get-tuple-element.16), channel_id=1, source_target_pairs={{0,3},{1,2},{2,1},{3,0},{4,7},{5,6},{6,5},{7,4},{8,11},{9,10},{10,... | collective-permute-start | bytes 196616 | tf_op jit(solution)/shard_map/ppermute | solution.py:72
  122.5 6.6 %collective-permute-start.3 = (f32[64,2,128]{2,0,1:T(8,128)S(1)}, f32[64,2,128]{2,0,1:T(8,128)S(1)}, u32[]{:S(2)}, u32[]{:S(2)}) collective-permute-start(f32[64,2,128]{2,0,1:T(8,128)S(1)} %get-tuple-element.17), channel_id=1, source_target_pairs={{0,4},{1,5},{2,6},{3,7},{4,0},{5,1},{6,2},{7,3},{8,12},{9,13},{10,... | collective-permute-start | bytes 196616 | tf_op jit(solution)/shard_map/ppermute | solution.py:72
  125.0 6.3 %collective-permute-start.5 = (f32[64,2,128]{2,0,1:T(8,128)S(1)}, f32[64,2,128]{2,0,1:T(8,128)S(1)}, u32[]{:S(2)}, u32[]{:S(2)}) collective-permute-start(f32[64,2,128]{2,0,1:T(8,128)S(1)} %get-tuple-element.18), channel_id=1, source_target_pairs={{0,6},{1,7},{2,4},{3,5},{4,2},{5,3},{6,0},{7,1},{8,14},{9,15},{10,... | collective-permute-start | bytes 196616 | tf_op jit(solution)/shard_map/ppermute | solution.py:72
  128.2 5.6 %collective-permute-start.6 = (f32[64,2,128]{2,0,1:T(8,128)S(1)}, f32[64,2,128]{2,0,1:T(8,128)S(1)}, u32[]{:S(2)}, u32[]{:S(2)}) collective-permute-start(f32[64,2,128]{2,0,1:T(8,128)S(1)} %get-tuple-element.12), channel_id=1, source_target_pairs={{0,7},{1,6},{2,5},{3,4},{4,3},{5,2},{6,1},{7,0},{8,15},{9,14},{10,... | collective-permute-start | bytes 196616 | tf_op jit(solution)/shard_map/ppermute | solution.py:72
Sparse Core Ops, SparseCore 0:
  56.1 35.6 reduce-scatter.1
